TPU v7x, 512 devices: a whole 4x8x8 slice. The times are simulated.
512 devices in a mesh: slab: 128 (over z, y, core), chan: 4 (over x).
Axes of the slice: x: 4, y: 8, z: 8, core: 2. Of those that a mesh axis runs over, the one named last changes fastest.
Arguments:
- field: bfloat16 [64, 256, 4096], P(None, 'slab'), may hold values from -6 to 6
- cotangent: bfloat16 [64, 256, 4096], P(None, 'slab'), may hold values from -10 to 10
- spectral_weight: bfloat16 [2, 64, 64, 512, 32], P(None, 'chan', None, 'slab'), may hold values from -4 to 4
- point_weight: bfloat16 [64, 64], replicated, may hold values from -0.75 to 0.75
- point_bias: bfloat16 [64], replicated, may hold values from -2 to 2
Outputs:
- grad_input: bfloat16 [64, 256, 4096], P('chan', 'slab')
- grad_spectral: float32 [2, 64, 64, 512, 32], P(None, 'chan', None, 'slab')
- grad_pointwise: float32 [64, 64], P('chan')
- grad_bias: float32 [64], replicated
All inputs are finite; a program needn't handle non-finite values.
Results may differ from a plain program's by a relative error of at most 0.023.
Values may be sent and summed in bfloat16 or wider, within the bound.
No kernel may reach another device: no remote copies, remote signals or barrier semaphores. Data moves between devices by JAX's collectives and lax.ppermute only.
A program may use at most 64 MiB of HBM per device.

v0:
```python
import math
import jax
import jax.numpy as jnp
from jax import lax
from jax.sharding import PartitionSpec as P

MX = 32
MY = 32
MZ = 16
NX = 256
NY = 64
NZ = 64


def kept_modes(total, length):
    mode_index = jnp.arange(total, dtype=jnp.int32)
    return jnp.where(mode_index < total // 2, mode_index, mode_index - total + length)


def phases(frequency, length):
    positions = jnp.arange(length, dtype=jnp.int32)
    wound_up = frequency[:, None] * positions[None, :] % length
    return 2.0 * math.pi / length * wound_up.astype(jnp.float32)


def make_tables():
    angle_z = phases(jnp.arange(MZ, dtype=jnp.int32), NZ)
    cosine_z = jnp.cos(angle_z)
    sine_z = jnp.sin(angle_z)
    forward_z = jnp.stack([cosine_z.T, -sine_z.T], 1).astype(jnp.bfloat16)
    weight_z = (jnp.where(jnp.arange(MZ) == 0, 1.0, 2.0) / (NX * NY * NZ)).astype(jnp.float32)
    scaled_z = jnp.stack([weight_z[:, None] * cosine_z, -weight_z[:, None] * sine_z], 1).astype(
        jnp.bfloat16
    )
    plain_z = jnp.stack([cosine_z, -sine_z], 1).astype(jnp.bfloat16)
    angle_y = phases(kept_modes(MY, NY), NY)
    cosine_y = jnp.cos(angle_y)
    sine_y = jnp.sin(angle_y)
    upper_rows = jnp.stack([cosine_y.T, -sine_y.T], -1)
    lower_rows = jnp.stack([sine_y.T, cosine_y.T], -1)
    forward_y = jnp.stack([upper_rows, lower_rows], 0).reshape(2 * NY, 2 * MY).astype(jnp.bfloat16)
    real_rows = jnp.stack([cosine_y, sine_y], 1)
    imag_rows = jnp.stack([-sine_y, cosine_y], 1)
    inverse_y = jnp.stack([real_rows, imag_rows], 1).reshape(2 * MY, 2 * NY).astype(jnp.bfloat16)
    angle_x = phases(kept_modes(MX, NX), NX)
    cosine_x = jnp.cos(angle_x).T.astype(jnp.bfloat16)
    sine_x = jnp.sin(angle_x).T.astype(jnp.bfloat16)
    return (forward_z, scaled_z, plain_z, forward_y, inverse_y, cosine_x, sine_x)


def to_modes(field_part, tables):
    forward_z, scaled_z, plain_z, forward_y, inverse_y, cosine_x, sine_x = tables
    channels = field_part.shape[0]
    planes = field_part.shape[1]
    grid_view = field_part.reshape(channels, planes, NY, NZ)
    section_one = jnp.einsum(
        "cxyz,zpk->cxkpy", grid_view, forward_z, preferred_element_type=jnp.float32
    ).astype(jnp.bfloat16)
    section_one = section_one.reshape(channels, planes, MZ, 2 * NY)
    section_two = jnp.einsum(
        "cxkm,mn->cxkn", section_one, forward_y, preferred_element_type=jnp.float32
    ).astype(jnp.bfloat16)
    section_two = section_two.reshape(channels, planes, 2 * MZ * MY)
    pencils = lax.all_to_all(section_two, "slab", split_axis=2, concat_axis=1, tiled=True)
    pencils = pencils.reshape(channels, NX, -1, 2)
    along_cos = jnp.einsum("cxmq,xk->cmqk", pencils, cosine_x, preferred_element_type=jnp.float32)
    along_sin = jnp.einsum("cxmq,xk->cmqk", pencils, sine_x, preferred_element_type=jnp.float32)
    real_part = along_cos[:, :, 0] + along_sin[:, :, 1]
    imag_part = along_cos[:, :, 1] - along_sin[:, :, 0]
    return jnp.stack([real_part, imag_part], 2)


def to_grid(spectra, tables, table_z):
    forward_z, scaled_z, plain_z, forward_y, inverse_y, cosine_x, sine_x = tables
    channels = spectra.shape[0]
    back_cos = jnp.einsum("cmqk,xk->cxmq", spectra, cosine_x, preferred_element_type=jnp.float32)
    back_sin = jnp.einsum("cmqk,xk->cxmq", spectra, sine_x, preferred_element_type=jnp.float32)
    real_part = back_cos[..., 0] - back_sin[..., 1]
    imag_part = back_cos[..., 1] + back_sin[..., 0]
    pencil_rows = jnp.stack([real_part, imag_part], -1).astype(jnp.bfloat16)
    pencil_rows = pencil_rows.reshape(channels, NX, -1)
    slabs = lax.all_to_all(pencil_rows, "slab", split_axis=1, concat_axis=2, tiled=True)
    channels = slabs.shape[0]
    planes = slabs.shape[1]
    slabs = slabs.reshape(channels, planes, MZ, 2 * MY)
    section_two = jnp.einsum(
        "cxkn,nm->cxkm", slabs, inverse_y, preferred_element_type=jnp.float32
    ).astype(jnp.bfloat16)
    section_two = section_two.reshape(channels, planes, MZ, 2, NY)
    grid_view = jnp.einsum(
        "cxkpy,kpz->cxyz", section_two, table_z, preferred_element_type=jnp.float32
    )
    return grid_view.reshape(channels, planes, NY * NZ)


def gelu_grad(pre_act):
    normal_cdf = 0.5 * (1.0 + jax.scipy.special.erf(pre_act / math.sqrt(2.0)))
    normal_pdf = jnp.exp(-0.5 * pre_act * pre_act) / math.sqrt(2.0 * math.pi)
    return normal_cdf + pre_act * normal_pdf


def body(field, cotangent, spectral_weight, point_weight, point_bias):
    tables = make_tables()
    scaled_z = tables[1]
    plain_z = tables[2]
    group_size = spectral_weight.shape[1]
    modes_dev = spectral_weight.shape[3]
    chan_start = lax.axis_index("chan") * group_size
    own_field = lax.dynamic_slice_in_dim(field, chan_start, group_size, 0)
    coeff = to_modes(own_field, tables).astype(jnp.bfloat16)
    coeff_real = coeff[:, :, 0]
    coeff_imag = coeff[:, :, 1]
    real_weight = spectral_weight[0]
    imag_weight = spectral_weight[1]
    spec_real = jnp.einsum(
        "imk,iomk->omk", coeff_real, real_weight, preferred_element_type=jnp.float32
    ) - jnp.einsum("imk,iomk->omk", coeff_imag, imag_weight, preferred_element_type=jnp.float32)
    spec_imag = jnp.einsum(
        "imk,iomk->omk", coeff_real, imag_weight, preferred_element_type=jnp.float32
    ) + jnp.einsum("imk,iomk->omk", coeff_imag, real_weight, preferred_element_type=jnp.float32)
    partial_spectra = jnp.stack([spec_real, spec_imag], 2)
    spectra = lax.psum(partial_spectra.astype(jnp.bfloat16), "chan")
    shaped = to_grid(spectra, tables, scaled_z)
    mixed = jnp.einsum("io,ixc->oxc", point_weight, field, preferred_element_type=jnp.float32)
    pre_act = shaped + mixed + point_bias.astype(jnp.float32)[:, None, None]
    grad_pre = (cotangent.astype(jnp.float32) * gelu_grad(pre_act)).astype(jnp.bfloat16)
    mode_index = lax.axis_index("slab") * modes_dev + jnp.arange(modes_dev, dtype=jnp.int32)
    mode_scale = (jnp.where(mode_index // MY == 0, 1.0, 2.0) / (NX * NY * NZ)).astype(jnp.float32)
    grad_hat = (to_modes(grad_pre, tables) * mode_scale[None, :, None, None]).astype(jnp.bfloat16)
    grad_real = grad_hat[:, :, 0]
    grad_imag = grad_hat[:, :, 1]
    outer_real = jnp.einsum(
        "imk,omk->iomk", coeff_real, grad_real, preferred_element_type=jnp.float32
    ) + jnp.einsum("imk,omk->iomk", coeff_imag, grad_imag, preferred_element_type=jnp.float32)
    outer_imag = jnp.einsum(
        "imk,omk->iomk", coeff_real, grad_imag, preferred_element_type=jnp.float32
    ) - jnp.einsum("imk,omk->iomk", coeff_imag, grad_real, preferred_element_type=jnp.float32)
    grad_spectral = jnp.stack([outer_real, outer_imag], 0)
    adj_real = jnp.einsum(
        "omk,iomk->imk", grad_real, real_weight, preferred_element_type=jnp.float32
    ) + jnp.einsum("omk,iomk->imk", grad_imag, imag_weight, preferred_element_type=jnp.float32)
    adj_imag = jnp.einsum(
        "omk,iomk->imk", grad_imag, real_weight, preferred_element_type=jnp.float32
    ) - jnp.einsum("omk,iomk->imk", grad_real, imag_weight, preferred_element_type=jnp.float32)
    adjoint = jnp.stack([adj_real, adj_imag], 2).astype(jnp.bfloat16)
    spectral_back = to_grid(adjoint, tables, plain_z)
    own_rows = lax.dynamic_slice_in_dim(point_weight, chan_start, group_size, 0)
    point_back = jnp.einsum("io,oxc->ixc", own_rows, grad_pre, preferred_element_type=jnp.float32)
    grad_input = (spectral_back + point_back).astype(jnp.bfloat16)
    inverse_root = 1.0 / math.sqrt(NX * NY * NZ)
    weight_part = (
        jnp.einsum("ixc,oxc->io", own_field, grad_pre, preferred_element_type=jnp.float32)
        * inverse_root
    )
    bias_part = jnp.sum(grad_pre, axis=(1, 2), dtype=jnp.float32) * inverse_root
    grad_pointwise, grad_bias = lax.psum((weight_part, bias_part), "slab")
    return (grad_input, grad_spectral, grad_pointwise, grad_bias)


def solution(mesh):
    placed = (
        P(None, "slab", None),
        P(None, "slab", None),
        P(None, "chan", None, "slab", None),
        P(),
        P(),
    )
    return jax.shard_map(
        body,
        mesh=mesh,
        in_specs=placed,
        out_specs=(
            P("chan", "slab", None),
            P(None, "chan", None, "slab", None),
            P("chan", None),
            P(),
        ),
        check_vma=False,
    )
```

profile of v0, /device:TPU:1, one launch (start us, length us, event | category | flops | bytes accessed | tf_op | source)
XLA Modules:
  0.0 397.6 jit_solution(5632324393416578759)
XLA Ops:
  1.1 1.8 copy.125
  2.9 0.3 copy.126
  3.2 0.3 reshape.577
  3.6 0.6 fusion.17
  4.1 0.3 copy.127
  4.6 0.2 convolution_convert_fusion.4
  4.8 0.5 copy.181
  5.2 1.0 reshape.605
  6.2 18.4 %all-to-all-start = ((bf16[128,2,128]{2,1,0:T(2,128)(2,1)}), bf16[128,2,128]{2,1,0:T(2,128)(2,1)S(1)}, u32[]{:S(2)}, u32[]{:S(2)}) async-start(bf16[128,2,128]{2,1,0:T(2,128)(2,1)} %reshape.605), calls=%async_computation | async-start | bytes 131072 | tf_op jit(solution)/shard_map/all_to_all | solution.py:64
  25.2 10.9 %all-to-all-done = bf16[128,2,128]{2,1,0:T(2,128)(2,1)S(1)} async-done(((bf16[128,2,128]{2,1,0:T(2,128)(2,1)}), bf16[128,2,128]{2,1,0:T(2,128)(2,1)S(1)}, u32[]{:S(2)}, u32[]{:S(2)}) %all-to-all-start) | async-done | bytes 65568 | tf_op jit(solution)/shard_map/all_to_all | solution.py:64
  36.0 0.4 reshape.606
  36.6 0.4 copy.132
  37.0 0.3 fusion.81
  37.3 0.3 fusion.87
  37.9 0.4 fusion.34
  38.4 0.4 fusion.24
  38.8 0.4 fusion.26
  39.2 0.4 fusion.32
  39.8 13.8 %psum.21 = bf16[64,4,2,32]{0,3,2,1:T(8,128)(2,1)S(1)} all-reduce(bf16[64,4,2,32]{0,3,2,1:T(8,128)(2,1)S(1)} %pad_maximum_fusion.2), channel_id=1, replica_groups=mesh['slab'=128,'chan'=4] {'chan'}, use_global_device_ids=true, to_apply=%region_0.1 | all-reduce | flops 16384 | bytes 65536 | tf_op jit(solution)/shard_map/psum | solution.py:122
  53.5 0.4 convolution_bitcast_fusion.3
  53.9 0.4 convolution_bitcast_fusion.2
  54.5 0.3 copy.134
  54.8 1.0 reshape.607
  55.8 9.5 %all-to-all-start.1 = ((bf16[128,2,512]{2,1,0:T(2,128)(2,1)}), bf16[128,2,512]{2,1,0:T(2,128)(2,1)S(1)}, u32[]{:S(2)}, u32[]{:S(2)}) async-start(bf16[128,2,512]{2,1,0:T(2,128)(2,1)} %reshape.607), calls=%async_computation.1 | async-start | bytes 524288 | tf_op jit(solution)/shard_map/all_to_all | solution.py:82
  65.5 15.2 %all-to-all-done.1 = bf16[128,2,512]{2,1,0:T(2,128)(2,1)S(1)} async-done(((bf16[128,2,512]{2,1,0:T(2,128)(2,1)}), bf16[128,2,512]{2,1,0:T(2,128)(2,1)S(1)}, u32[]{:S(2)}, u32[]{:S(2)}) %all-to-all-start.1) | async-done | bytes 262176 | tf_op jit(solution)/shard_map/all_to_all | solution.py:82
  80.7 0.3 reshape.608
  81.0 0.8 copy.137
  81.8 0.3 convolution_convert_fusion.1
  82.1 0.4 reshape.567
  82.5 2.7 convolution_bitcast_fusion
  85.2 4.2 %reshape.568 = f32[64,2,4096]{2,1,0:T(2,128)S(1)} reshape(f32[64,2,64,64]{3,2,1,0:T(8,128)} %convolution_bitcast_fusion) | data formatting | bytes 4194304 | tf_op jit(solution)/shard_map/reshape | solution.py:93
  89.4 5.7 %convert_reduce_fusion = (f32[64]{0:T(128)S(1)}, bf16[64,2,4096]{2,0,1:T(8,128)(2,1)S(1)}) fusion(f32[64]{0:T(128)S(1)} %convert_element_type.232, bf16[64,2,4096]{2,1,0:T(2,128)(2,1)} %param.5, bf16[64,64]{1,0:T(8,128)(2,1)S(1)} %copy-done, f32[64,2,4096]{2,1,0:T(2,128)S(1)} %reshape.568, bf16[64,2,4096]{2,1,0:T(2,128)(2,1)} %param.6), kind=kOutput, calls=%fused_computation.16 | convolution fusion | flops 74973120 | bytes 5251584 | tf_op jit(solution)/shard_map/io,ixc->oxc/dot_general | solution.py:124
  95.1 2.3 reshape.569
  97.4 2.0 fusion.14
  99.4 1.6 copy.143
  101.1 0.5 reshape.570
  101.6 0.3 convolution_convert_fusion
  101.9 0.7 copy.183
  102.6 1.0 reshape.609
  103.6 5.8 %all-to-all-start.2 = ((bf16[128,2,512]{2,1,0:T(2,128)(2,1)}), bf16[128,2,512]{2,1,0:T(2,128)(2,1)S(1)}, u32[]{:S(2)}, u32[]{:S(2)}) async-start(bf16[128,2,512]{2,1,0:T(2,128)(2,1)} %reshape.609), calls=%async_computation.2 | async-start | bytes 524288 | tf_op jit(solution)/shard_map/all_to_all | solution.py:64
  109.4 0.4 fusion.18
  109.8 256.7 %all-reduce = (f32[16,64]{1,0:T(8,128)}, f32[64]{0:T(128)}) all-reduce(f32[16,64]{1,0:T(8,128)S(1)} %fusion.18, f32[64]{0:T(128)S(1)} %broadcast_multiply_fusion), channel_id=1, replica_groups=mesh['slab'=128,'chan'=4] {'slab'}, use_global_device_ids=true, to_apply=%region_1.2 | all-reduce | flops 1088 | bytes 8704 | tf_op jit(solution)/shard_map/psum | solution.py:156
  366.5 0.3 reshape.610
  367.0 0.5 copy.147
  367.6 0.3 fusion.84
  367.9 0.3 fusion.78
  368.4 0.4 fusion.22
  368.8 0.4 fusion.28
  369.2 0.4 fusion.30
  369.7 0.4 fusion.20
  370.5 0.3 convolution_bitcast_fusion.5
  370.8 0.3 convolution_bitcast_fusion.4
  371.2 0.3 copy.149
  371.5 1.0 reshape.611
  372.5 10.4 %all-to-all-start.3 = ((bf16[128,2,128]{2,1,0:T(2,128)(2,1)}), bf16[128,2,128]{2,1,0:T(2,128)(2,1)S(1)}, u32[]{:S(2)}, u32[]{:S(2)}) async-start(bf16[128,2,128]{2,1,0:T(2,128)(2,1)} %reshape.611), calls=%async_computation.3 | async-start | bytes 131072 | tf_op jit(solution)/shard_map/all_to_all | solution.py:82
  382.9 0.6 add_bitcast_fusion
  383.5 1.6 pad_maximum_fusion
  385.1 9.2 %all-to-all-done.3 = bf16[128,2,128]{2,1,0:T(2,128)(2,1)S(1)} async-done(((bf16[128,2,128]{2,1,0:T(2,128)(2,1)}), bf16[128,2,128]{2,1,0:T(2,128)(2,1)S(1)}, u32[]{:S(2)}, u32[]{:S(2)}) %all-to-all-start.3) | async-done | bytes 65568 | tf_op jit(solution)/shard_map/all_to_all | solution.py:82
  394.3 0.4 reshape.612
  394.7 0.3 copy.151
  395.3 0.3 convolution_bitcast_fusion.1
  395.7 0.5 reshape.575
  396.2 0.4 fusion.1
  396.6 1.0 copy.156
  (67 shorter events, 2.9 us)
Async XLA Ops:
  0.6 88.8 %copy-start = (bf16[64,64]{1,0:T(8,128)(2,1)S(1)}, bf16[64,64]{1,0:T(8,128)(2,1)}, u32[]{:S(2)}) copy-start(bf16[64,64]{1,0:T(8,128)(2,1)} %param.8) | copy-start | bytes 24580
  3.2 21.6 %copy-start.1 = (bf16[2,16,64,4,32]{2,4,3,1,0:T(8,128)(2,1)S(1)}, bf16[2,16,64,4,32]{2,4,3,1,0:T(8,128)(2,1)}, u32[]{:S(2)}) copy-start(bf16[2,16,64,4,32]{2,4,3,1,0:T(8,128)(2,1)} %param.7) | copy-start | bytes 1572868
  4.6 20.5 %copy-start.6 = (bf16[64]{0:T(256)(128)(2,1)S(1)}, bf16[64]{0:T(256)(128)(2,1)}, u32[]{:S(2)}) copy-start(bf16[64]{0:T(256)(128)(2,1)} %param.9) | copy-start | bytes 388
  6.2 29.8 %all-to-all-start = ((bf16[128,2,128]{2,1,0:T(2,128)(2,1)}), bf16[128,2,128]{2,1,0:T(2,128)(2,1)S(1)}, u32[]{:S(2)}, u32[]{:S(2)}) async-start(bf16[128,2,128]{2,1,0:T(2,128)(2,1)} %reshape.605), calls=%async_computation | async-start | bytes 131072 | tf_op jit(solution)/shard_map/all_to_all | solution.py:64
  24.9 13.9 %copy-start.2 = (bf16[16,64,4,32]{1,3,2,0:T(8,128)(2,1)}, bf16[16,64,4,32]{1,3,2,0:T(8,128)(2,1)S(1)}, u32[]{:S(2)}) copy-start(bf16[16,64,4,32]{1,3,2,0:T(8,128)(2,1)S(1)} %get-tuple-element.33) | copy-start | bytes 786436
  24.9 14.3 %copy-start.4 = (bf16[16,64,4,32]{1,3,2,0:T(8,128)(2,1)}, bf16[16,64,4,32]{1,3,2,0:T(8,128)(2,1)S(1)}, u32[]{:S(2)}) copy-start(bf16[16,64,4,32]{1,3,2,0:T(8,128)(2,1)S(1)} %get-tuple-element.32) | copy-start | bytes 786436
  55.8 24.8 %all-to-all-start.1 = ((bf16[128,2,512]{2,1,0:T(2,128)(2,1)}), bf16[128,2,512]{2,1,0:T(2,128)(2,1)S(1)}, u32[]{:S(2)}, u32[]{:S(2)}) async-start(bf16[128,2,512]{2,1,0:T(2,128)(2,1)} %reshape.607), calls=%async_computation.1 | async-start | bytes 524288 | tf_op jit(solution)/shard_map/all_to_all | solution.py:82
  103.6 262.9 %all-to-all-start.2 = ((bf16[128,2,512]{2,1,0:T(2,128)(2,1)}), bf16[128,2,512]{2,1,0:T(2,128)(2,1)S(1)}, u32[]{:S(2)}, u32[]{:S(2)}) async-start(bf16[128,2,512]{2,1,0:T(2,128)(2,1)} %reshape.609), calls=%async_computation.2 | async-start | bytes 524288 | tf_op jit(solution)/shard_map/all_to_all | solution.py:64
  366.8 1.5 copy-start.3
  366.9 1.9 copy-start.5
  372.5 21.8 %all-to-all-start.3 = ((bf16[128,2,128]{2,1,0:T(2,128)(2,1)}), bf16[128,2,128]{2,1,0:T(2,128)(2,1)S(1)}, u32[]{:S(2)}, u32[]{:S(2)}) async-start(bf16[128,2,128]{2,1,0:T(2,128)(2,1)} %reshape.611), calls=%async_computation.3 | async-start | bytes 131072 | tf_op jit(solution)/shard_map/all_to_all | solution.py:82
where the time goes:
time: 398 us
  blocking collectives  270 us (68%)
  starting transfers between devices  44.1 us (11%)
  waiting for transfers between devices  35.3 us (9%)
  local copies, waits for them, and re-layouts  24 us (6%)
  matrix products  19.2 us (5%)
    psum x1, blocking collectives, body(): grad_pointwise, grad_bias = lax.psum((weight_part, bias_part), 'slab')  257 us
    all_to_all x2, waiting for transfers between devices, to_grid(): lax.all_to_all(pencil_rows, 'slab', split_axis=1, concat_axis=2, tiled=True)  24.4 us
    all_to_all x2, starting transfers between devices, to_modes(): lax.all_to_all(section_two, 'slab', split_axis=2, concat_axis=1, tiled=True)  24.2 us
    all_to_all x2, starting transfers between devices, to_grid(): lax.all_to_all(pencil_rows, 'slab', split_axis=1, concat_axis=2, tiled=True)  19.9 us
    psum x1, blocking collectives, body(): spectra = lax.psum(partial_spectra.astype(jnp.bfloat16), 'chan')  13.8 us
    all_to_all x2, waiting for transfers between devices, to_modes(): lax.all_to_all(section_two, 'slab', split_axis=2, concat_axis=1, tiled=True)  10.9 us
    unnamed x24, local copies, waits for them, and re-layouts  8.16 us
  transfers between devices with their start and end apart: 4, of which 3 were waited for; matrix products, arithmetic and copies ran while one was open for 1% of the time, Pallas kernels for 0%

commit v1 on v0

--- a/solution.py
+++ b/solution.py
@@ -119,7 +119,7 @@
         "imk,iomk->omk", coeff_real, imag_weight, preferred_element_type=jnp.float32
     ) + jnp.einsum("imk,iomk->omk", coeff_imag, real_weight, preferred_element_type=jnp.float32)
     partial_spectra = jnp.stack([spec_real, spec_imag], 2)
-    spectra = lax.psum(partial_spectra.astype(jnp.bfloat16), "chan")
+    spectra = jnp.sum(lax.all_gather(partial_spectra.astype(jnp.bfloat16), "chan"), axis=0)
     shaped = to_grid(spectra, tables, scaled_z)
     mixed = jnp.einsum("io,ixc->oxc", point_weight, field, preferred_element_type=jnp.float32)
     pre_act = shaped + mixed + point_bias.astype(jnp.float32)[:, None, None]

time: 398 us -> 393 us (0.987)
    psum x1 -> x0, blocking collectives: 13.8 us -> none  [body(): spectra = lax.psum(partial_spectra.astype(jnp.bfloat16), 'chan')]
    all_gather x0 -> x1, blocking collectives: none -> 10.1 us  [body(): lax.all_gather(partial_spectra.astype(jnp.bfloat16), 'chan')]
where the time goes in v1:
time: 393 us
  blocking collectives  267 us (68%)
  starting transfers between devices  42.9 us (11%)
  waiting for transfers between devices  35.3 us (9%)
  local copies, waits for them, and re-layouts  24 us (6%)
  matrix products  19.2 us (5%)
    psum x1, blocking collectives, body(): grad_pointwise, grad_bias = lax.psum((weight_part, bias_part), 'slab')  257 us
    all_to_all x2, waiting for transfers between devices, to_grid(): lax.all_to_all(pencil_rows, 'slab', split_axis=1, concat_axis=2, tiled=True)  24.4 us
    all_to_all x2, starting transfers between devices, to_modes(): lax.all_to_all(section_two, 'slab', split_axis=2, concat_axis=1, tiled=True)  24.2 us
    all_to_all x2, starting transfers between devices, to_grid(): lax.all_to_all(pencil_rows, 'slab', split_axis=1, concat_axis=2, tiled=True)  18.7 us
    all_to_all x2, waiting for transfers between devices, to_modes(): lax.all_to_all(section_two, 'slab', split_axis=2, concat_axis=1, tiled=True)  10.9 us
    all_gather x1, blocking collectives, body(): lax.all_gather(partial_spectra.astype(jnp.bfloat16), 'chan')  10.1 us
    unnamed x24, local copies, waits for them, and re-layouts  8.17 us
  transfers between devices with their start and end apart: 4, of which 3 were waited for; matrix products, arithmetic and copies ran while one was open for 1% of the time, Pallas kernels for 0%

profile of v1, /device:TPU:1, one launch (start us, length us, event | category | flops | bytes accessed | tf_op | source)
XLA Modules:
  0.0 392.8 jit_solution(692338109514496224)
XLA Ops:
  1.1 1.8 copy.125
  2.9 0.3 copy.126
  3.2 0.3 reshape.610
  3.6 0.6 fusion.17
  4.1 0.3 copy.127
  4.6 0.2 convolution_convert_fusion.4
  4.8 0.5 copy.181
  5.2 1.0 reshape.638
  6.2 18.4 %all-to-all-start = ((bf16[128,2,128]{2,1,0:T(2,128)(2,1)}), bf16[128,2,128]{2,1,0:T(2,128)(2,1)S(1)}, u32[]{:S(2)}, u32[]{:S(2)}) async-start(bf16[128,2,128]{2,1,0:T(2,128)(2,1)} %reshape.638), calls=%async_computation | async-start | bytes 131072 | tf_op jit(solution)/shard_map/all_to_all | solution.py:64
  25.1 10.9 %all-to-all-done = bf16[128,2,128]{2,1,0:T(2,128)(2,1)S(1)} async-done(((bf16[128,2,128]{2,1,0:T(2,128)(2,1)}), bf16[128,2,128]{2,1,0:T(2,128)(2,1)S(1)}, u32[]{:S(2)}, u32[]{:S(2)}) %all-to-all-start) | async-done | bytes 65568 | tf_op jit(solution)/shard_map/all_to_all | solution.py:64
  36.0 0.4 reshape.639
  36.6 0.4 copy.132
  37.0 0.3 fusion.81
  37.3 0.3 fusion.87
  37.9 0.4 fusion.34
  38.4 0.4 fusion.24
  38.8 0.4 fusion.26
  39.2 0.4 fusion.32
  39.7 10.1 %all_gather.4 = bf16[4,64,4,2,32]{1,4,3,2,0:T(8,128)(2,1)S(1)} all-gather(bf16[1,64,4,2,32]{1,4,3,2,0:T(8,128)(2,1)S(1)} %pad_maximum_fusion.2), channel_id=1, replica_groups=mesh['slab'=128,'chan'=4] {'chan'}, dimensions={0}, use_global_device_ids=true | all-gather | bytes 163840 | tf_op jit(solution)/shard_map/all_gather | solution.py:122
  49.9 0.4 convolution_bitcast_fusion.3
  50.3 0.4 convolution_bitcast_fusion.2
  50.8 0.3 copy.134
  51.1 1.0 reshape.640
  52.1 8.3 %all-to-all-start.1 = ((bf16[128,2,512]{2,1,0:T(2,128)(2,1)}), bf16[128,2,512]{2,1,0:T(2,128)(2,1)S(1)}, u32[]{:S(2)}, u32[]{:S(2)}) async-start(bf16[128,2,512]{2,1,0:T(2,128)(2,1)} %reshape.640), calls=%async_computation.1 | async-start | bytes 524288 | tf_op jit(solution)/shard_map/all_to_all | solution.py:82
  60.6 15.2 %all-to-all-done.1 = bf16[128,2,512]{2,1,0:T(2,128)(2,1)S(1)} async-done(((bf16[128,2,512]{2,1,0:T(2,128)(2,1)}), bf16[128,2,512]{2,1,0:T(2,128)(2,1)S(1)}, u32[]{:S(2)}, u32[]{:S(2)}) %all-to-all-start.1) | async-done | bytes 262176 | tf_op jit(solution)/shard_map/all_to_all | solution.py:82
  75.8 0.3 reshape.641
  76.2 0.8 copy.137
  77.0 0.3 convolution_convert_fusion.1
  77.3 0.4 reshape.600
  77.7 2.7 convolution_bitcast_fusion
  80.4 4.2 %reshape.601 = f32[64,2,4096]{2,1,0:T(2,128)S(1)} reshape(f32[64,2,64,64]{3,2,1,0:T(8,128)} %convolution_bitcast_fusion) | data formatting | bytes 4194304 | tf_op jit(solution)/shard_map/reshape | solution.py:93
  84.6 5.7 %convert_reduce_fusion = (f32[64]{0:T(128)S(1)}, bf16[64,2,4096]{2,0,1:T(8,128)(2,1)S(1)}) fusion(f32[64]{0:T(128)S(1)} %convert_element_type.241, bf16[64,2,4096]{2,1,0:T(2,128)(2,1)} %param.5, bf16[64,64]{1,0:T(8,128)(2,1)S(1)} %copy-done, f32[64,2,4096]{2,1,0:T(2,128)S(1)} %reshape.601, bf16[64,2,4096]{2,1,0:T(2,128)(2,1)} %param.6), kind=kOutput, calls=%fused_computation.16 | convolution fusion | flops 74973120 | bytes 5251584 | tf_op jit(solution)/shard_map/io,ixc->oxc/dot_general | solution.py:124
  90.3 2.3 reshape.602
  92.6 2.0 fusion.14
  94.6 1.6 copy.143
  96.2 0.5 reshape.603
  96.7 0.3 convolution_convert_fusion
  97.0 0.7 copy.183
  97.7 1.0 reshape.642
  98.7 5.8 %all-to-all-start.2 = ((bf16[128,2,512]{2,1,0:T(2,128)(2,1)}), bf16[128,2,512]{2,1,0:T(2,128)(2,1)S(1)}, u32[]{:S(2)}, u32[]{:S(2)}) async-start(bf16[128,2,512]{2,1,0:T(2,128)(2,1)} %reshape.642), calls=%async_computation.2 | async-start | bytes 524288 | tf_op jit(solution)/shard_map/all_to_all | solution.py:64
  104.6 0.4 fusion.18
  105.0 256.7 %all-reduce = (f32[16,64]{1,0:T(8,128)}, f32[64]{0:T(128)}) all-reduce(f32[16,64]{1,0:T(8,128)S(1)} %fusion.18, f32[64]{0:T(128)S(1)} %broadcast_multiply_fusion), channel_id=1, replica_groups=mesh['slab'=128,'chan'=4] {'slab'}, use_global_device_ids=true, to_apply=%region_1.2 | all-reduce | flops 1088 | bytes 8704 | tf_op jit(solution)/shard_map/psum | solution.py:156
  361.6 0.3 reshape.643
  362.2 0.5 copy.147
  362.7 0.3 fusion.84
  363.0 0.3 fusion.78
  363.5 0.4 fusion.22
  363.9 0.4 fusion.28
  364.4 0.4 fusion.30
  364.8 0.4 fusion.20
  365.6 0.3 convolution_bitcast_fusion.5
  365.9 0.3 convolution_bitcast_fusion.4
  366.3 0.3 copy.149
  366.7 1.0 reshape.644
  367.6 10.4 %all-to-all-start.3 = ((bf16[128,2,128]{2,1,0:T(2,128)(2,1)}), bf16[128,2,128]{2,1,0:T(2,128)(2,1)S(1)}, u32[]{:S(2)}, u32[]{:S(2)}) async-start(bf16[128,2,128]{2,1,0:T(2,128)(2,1)} %reshape.644), calls=%async_computation.3 | async-start | bytes 131072 | tf_op jit(solution)/shard_map/all_to_all | solution.py:82
  378.0 0.6 add_bitcast_fusion
  378.7 1.6 pad_maximum_fusion
  380.2 9.2 %all-to-all-done.3 = bf16[128,2,128]{2,1,0:T(2,128)(2,1)S(1)} async-done(((bf16[128,2,128]{2,1,0:T(2,128)(2,1)}), bf16[128,2,128]{2,1,0:T(2,128)(2,1)S(1)}, u32[]{:S(2)}, u32[]{:S(2)}) %all-to-all-start.3) | async-done | bytes 65568 | tf_op jit(solution)/shard_map/all_to_all | solution.py:82
  389.5 0.4 reshape.645
  389.9 0.3 copy.151
  390.5 0.3 convolution_bitcast_fusion.1
  390.8 0.5 reshape.608
  391.4 0.4 fusion.1
  391.8 1.0 copy.156
  (68 shorter events, 2.9 us)
Async XLA Ops:
  0.6 84.0 %copy-start = (bf16[64,64]{1,0:T(8,128)(2,1)S(1)}, bf16[64,64]{1,0:T(8,128)(2,1)}, u32[]{:S(2)}) copy-start(bf16[64,64]{1,0:T(8,128)(2,1)} %param.8) | copy-start | bytes 24580
  3.2 21.6 %copy-start.1 = (bf16[2,16,64,4,32]{2,4,3,1,0:T(8,128)(2,1)S(1)}, bf16[2,16,64,4,32]{2,4,3,1,0:T(8,128)(2,1)}, u32[]{:S(2)}) copy-start(bf16[2,16,64,4,32]{2,4,3,1,0:T(8,128)(2,1)} %param.7) | copy-start | bytes 1572868
  4.6 20.5 %copy-start.6 = (bf16[64]{0:T(256)(128)(2,1)S(1)}, bf16[64]{0:T(256)(128)(2,1)}, u32[]{:S(2)}) copy-start(bf16[64]{0:T(256)(128)(2,1)} %param.9) | copy-start | bytes 388
  6.2 29.8 %all-to-all-start = ((bf16[128,2,128]{2,1,0:T(2,128)(2,1)}), bf16[128,2,128]{2,1,0:T(2,128)(2,1)S(1)}, u32[]{:S(2)}, u32[]{:S(2)}) async-start(bf16[128,2,128]{2,1,0:T(2,128)(2,1)} %reshape.638), calls=%async_computation | async-start | bytes 131072 | tf_op jit(solution)/shard_map/all_to_all | solution.py:64
  24.9 13.9 %copy-start.2 = (bf16[16,64,4,32]{1,3,2,0:T(8,128)(2,1)}, bf16[16,64,4,32]{1,3,2,0:T(8,128)(2,1)S(1)}, u32[]{:S(2)}) copy-start(bf16[16,64,4,32]{1,3,2,0:T(8,128)(2,1)S(1)} %get-tuple-element.33) | copy-start | bytes 786436
  24.9 14.4 %copy-start.4 = (bf16[16,64,4,32]{1,3,2,0:T(8,128)(2,1)}, bf16[16,64,4,32]{1,3,2,0:T(8,128)(2,1)S(1)}, u32[]{:S(2)}) copy-start(bf16[16,64,4,32]{1,3,2,0:T(8,128)(2,1)S(1)} %get-tuple-element.32) | copy-start | bytes 786436
  52.1 23.6 %all-to-all-start.1 = ((bf16[128,2,512]{2,1,0:T(2,128)(2,1)}), bf16[128,2,512]{2,1,0:T(2,128)(2,1)S(1)}, u32[]{:S(2)}, u32[]{:S(2)}) async-start(bf16[128,2,512]{2,1,0:T(2,128)(2,1)} %reshape.640), calls=%async_computation.1 | async-start | bytes 524288 | tf_op jit(solution)/shard_map/all_to_all | solution.py:82
  98.7 262.9 %all-to-all-start.2 = ((bf16[128,2,512]{2,1,0:T(2,128)(2,1)}), bf16[128,2,512]{2,1,0:T(2,128)(2,1)S(1)}, u32[]{:S(2)}, u32[]{:S(2)}) async-start(bf16[128,2,512]{2,1,0:T(2,128)(2,1)} %reshape.642), calls=%async_computation.2 | async-start | bytes 524288 | tf_op jit(solution)/shard_map/all_to_all | solution.py:64
  362.0 1.5 copy-start.3
  362.1 1.9 copy-start.5
  367.6 21.8 %all-to-all-start.3 = ((bf16[128,2,128]{2,1,0:T(2,128)(2,1)}), bf16[128,2,128]{2,1,0:T(2,128)(2,1)S(1)}, u32[]{:S(2)}, u32[]{:S(2)}) async-start(bf16[128,2,128]{2,1,0:T(2,128)(2,1)} %reshape.644), calls=%async_computation.3 | async-start | bytes 131072 | tf_op jit(solution)/shard_map/all_to_all | solution.py:82
